TPU v7x, 256 devices: a whole 4x4x8 slice. The times are simulated.
256 devices in a mesh: expert: 16 (over y_lo, x, core), dp: 16 (over y_hi, z).
Axes of the slice: x: 4, y: 4 (y_hi: 2, y_lo: 2; y = y_hi * 2 + y_lo), z: 8, core: 2. Of those that a mesh axis runs over, the one named last changes fastest.
Arguments:
- attn_input: bfloat16 [12288, 4096], P('dp'), may hold values from -6 to 6
- query_grad: bfloat16 [12288, 8192], P('dp', 'expert'), may hold values from -6 to 6
- query_weight: float32 [8192, 4096], P(('expert', 'dp')), may hold values from -40 to 40
- moe_cotangent: bfloat16 [2048, 4096], P('expert', 'dp'), may hold values from -6 to 6
- expert_ids: int32 [2048, 8], P('expert'), may hold values from 0 to 31, all different within a row; in each aligned block of 128 rows (0 to 127, 128 to 255, ...) at most 40 rows name the same one
- route_weights: float32 [2048, 8], P('expert'), may hold values from 0.2 to 1
- gate_saved: bfloat16 [640, 32, 1536], P('dp', 'expert'), may hold values from -6 to 6
- up_saved: bfloat16 [640, 32, 1536], P('dp', 'expert'), may hold values from -6 to 6
- gate_weight: bfloat16 [32, 4096, 1536], P('expert', 'dp'), may hold values from -0.09375 to 0.09375
- up_weight: bfloat16 [32, 4096, 1536], P('expert', 'dp'), may hold values from -0.09375 to 0.09375
- down_weight: bfloat16 [32, 1536, 4096], P('expert', None, 'dp'), may hold values from -0.15625 to 0.15625
Outputs:
- query_weight_next: float32 [8192, 4096], P(('expert', 'dp'))
- moe_input_grad: float32 [2048, 4096], P('expert', 'dp')
Inputs may be any that keep to these rules, and one draw needn't show every extreme that they name: `expert_ids`: in each aligned block of 128 rows no expert is named by more than 40 rows, and one expert by exactly 40 rows in some block; each row names 8 different experts.
All inputs are finite; a program needn't handle non-finite values.
Results may differ from a plain program's by a relative error of at most 0.022.
Values may be sent and summed in bfloat16 or wider, within the bound.
A program may use at most 128 MiB of HBM per device.

v0:
```python
import jax
import jax.numpy as jnp
from jax import lax
from jax.sharding import PartitionSpec as P

step_rate = 0.01
epsilon = 1e-06


def slot_tables(expert_ids, route_weights, experts, capacity):
    expert_iota = lax.broadcasted_iota(jnp.int32, (1, 1, experts), 2)
    chosen = (expert_ids[:, :, None] == expert_iota).astype(jnp.int32)
    counts = jnp.sum(chosen, axis=1, dtype=jnp.int32)
    rows = counts.shape[0]
    earlier = lax.broadcasted_iota(jnp.int32, (rows, rows), 1) < lax.broadcasted_iota(
        jnp.int32, (rows, rows), 0
    )
    before = jnp.dot(
        earlier.astype(jnp.bfloat16),
        counts.astype(jnp.bfloat16),
        preferred_element_type=jnp.float32,
    ).astype(jnp.int32)
    position = jnp.sum(chosen * before[:, None, :], axis=2, dtype=jnp.int32)
    slot_code = position * experts + expert_ids
    slot_iota = lax.broadcasted_iota(jnp.int32, (1, 1, capacity * experts), 2)
    matched = slot_code[:, :, None] == slot_iota
    select = jnp.sum(matched.astype(jnp.float32), axis=1)
    scaled = jnp.sum(jnp.where(matched, route_weights[:, :, None], 0.0), axis=1)
    return (select, scaled)


def activation_grads(hidden, gate_vals, up_vals):
    gate_float = gate_vals.astype(jnp.float32)
    up_float = up_vals.astype(jnp.float32)
    sigmoid_vals = jax.nn.sigmoid(gate_float)
    gate_grad = hidden * up_float * sigmoid_vals * (1.0 + gate_float * (1.0 - sigmoid_vals))
    up_grad = hidden * gate_float * sigmoid_vals
    return jnp.stack([gate_grad, up_grad], axis=2).astype(jnp.bfloat16)


def weight_update(attn_input, query_grad, query_weight):
    gradient = lax.psum_scatter(
        lax.dot_general(
            query_grad, attn_input, (((0,), (0,)), ((), ())), preferred_element_type=jnp.float32
        ).astype(jnp.bfloat16),
        "dp",
        scatter_dimension=0,
        tiled=True,
    ).astype(jnp.float32)
    radial = jnp.mean(query_weight * gradient, axis=1, keepdims=True) / (
        jnp.mean(query_weight * query_weight, axis=1, keepdims=True) + epsilon
    )
    stepped = query_weight - step_rate * (gradient - radial * query_weight)
    return stepped * lax.rsqrt(jnp.mean(stepped * stepped, axis=1, keepdims=True) + epsilon)


def expert_update(
    moe_cotangent,
    expert_ids,
    route_weights,
    gate_saved,
    up_saved,
    gate_weight,
    up_weight,
    down_weight,
):
    groups = lax.axis_size("expert")
    experts = gate_weight.shape[0] * groups
    capacity = gate_saved.shape[0] * lax.axis_size("dp") // groups
    select, scaled = slot_tables(expert_ids, route_weights, experts, capacity)
    outgoing = jnp.dot(
        scaled.T,
        moe_cotangent.astype(jnp.float32),
        precision=lax.Precision.HIGHEST,
        preferred_element_type=jnp.float32,
    )
    outgoing = outgoing.astype(jnp.bfloat16).reshape(capacity, experts, moe_cotangent.shape[1])
    arrived = lax.all_to_all(outgoing, "expert", split_axis=1, concat_axis=0, tiled=True)
    hidden = lax.psum_scatter(
        jnp.einsum("sec,ehc->seh", arrived, down_weight, preferred_element_type=jnp.float32).astype(
            jnp.bfloat16
        ),
        "dp",
        scatter_dimension=0,
        tiled=True,
    ).astype(jnp.float32)
    grads_pair = activation_grads(hidden, gate_saved, up_saved)
    part_rows = lax.all_gather(grads_pair, "dp", axis=0, tiled=True)
    total = jnp.einsum(
        "seh,ech->sec", part_rows[:, :, 0], gate_weight, preferred_element_type=jnp.float32
    )
    total = total + jnp.einsum(
        "seh,ech->sec", part_rows[:, :, 1], up_weight, preferred_element_type=jnp.float32
    )
    slot_input = total.astype(jnp.bfloat16)
    returned_rows = lax.all_to_all(slot_input, "expert", split_axis=0, concat_axis=1, tiled=True)
    flat_rows = returned_rows.reshape(capacity * experts, returned_rows.shape[2])
    return jnp.dot(select.astype(jnp.bfloat16), flat_rows, preferred_element_type=jnp.float32)


def shards(
    attn_input,
    query_grad,
    query_weight,
    moe_cotangent,
    expert_ids,
    route_weights,
    gate_saved,
    up_saved,
    gate_weight,
    up_weight,
    down_weight,
):
    moe_input_grad = expert_update(
        moe_cotangent,
        expert_ids,
        route_weights,
        gate_saved,
        up_saved,
        gate_weight,
        up_weight,
        down_weight,
    )
    query_weight_next = weight_update(attn_input, query_grad, query_weight)
    return (query_weight_next, moe_input_grad)


def solution(mesh):
    placed = (
        P("dp", None),
        P("dp", "expert"),
        P(("expert", "dp"), None),
        P("expert", "dp"),
        P("expert", None),
        P("expert", None),
        P("dp", "expert", None),
        P("dp", "expert", None),
        P("expert", "dp", None),
        P("expert", "dp", None),
        P("expert", None, "dp"),
    )
    return jax.shard_map(
        shards,
        mesh=mesh,
        in_specs=placed,
        out_specs=(P(("expert", "dp"), None), P("expert", "dp")),
        check_vma=False,
    )
```

profile of v0, /device:TPU:1, one launch (start us, length us, event | category | flops | bytes accessed | tf_op | source)
XLA Modules:
  0.0 630.1 jit_solution(1963007149182575208)
XLA Ops:
  7.2 0.0 copy-start
  7.2 0.0 reduce-scatter.7.cloned.1.call-start
  7.2 0.8 convert_reduce_fusion.1
  8.0 0.1 convolution_convert_fusion.3
  8.2 0.7 select_reduce_fusion.1
  8.9 0.7 multiply_add_fusion
  9.6 0.1 copy.38
  9.7 0.8 copy.39
  10.5 4.1 convert_reduce_fusion
  14.6 1.6 convolution_convert_fusion.2
  16.2 0.4 copy.40
  16.6 18.3 %all_to_all.33 = bf16[40,32,256]{2,0,1:T(8,128)(2,1)S(1)} all-to-all(bf16[40,32,256]{2,0,1:T(8,128)(2,1)S(1)} %copy.40), channel_id=1, replica_groups=mesh['expert'=16,'dp'=16] {'expert'}, dimensions={1} | all-to-all | bytes 1310720 | tf_op jit(solution)/shard_map/all_to_all | solution.py:78
  35.0 0.0 copy-done
  35.0 1.2 fusion.2
  36.2 2.5 copy.49
  38.7 0.0 copy-start.6
  38.7 0.0 reduce-scatter.7.cloned.1.call-update
  38.7 0.0 reduce-scatter.5.cloned.1.call-start
  38.7 1.1 copy-done.6
  39.8 7.8 %convolution_convert_fusion = bf16[512,4096]{1,0:T(8,128)(2,1)} fusion(bf16[768,512]{1,0:T(8,128)(2,1)S(1)} %copy-done.6, bf16[768,4096]{1,0:T(8,128)(2,1)} %param.11), kind=kOutput, calls=%fused_computation | convolution fusion | flops 3223322624 | bytes 11272192 | tf_op jit(solution)/shard_map/dot_general | solution.py:43
  47.6 0.0 copy-start.3
  47.6 0.0 copy-start.4
  47.6 0.0 copy-start.1
  47.6 0.0 reduce-scatter.5.cloned.1.call-update
  47.6 0.0 all-gather.2.cloned.1.call-start
  47.6 200.5 %reduce-scatter.7.cloned.1.call-done = bf16[40,3072]{1,0:T(8,128)(2,1)} async-done(((bf16[640,3072]{1,0:T(8,128)(2,1)}), bf16[40,3072]{1,0:T(8,128)(2,1)}) %reduce-scatter.7.cloned.1.call-update) | async-done | bytes 245776
  248.1 0.0 copy-done.3
  248.1 0.0 copy-done.4
  248.1 1.2 fusion.22
  249.3 0.8 pad_maximum_fusion
  250.1 0.0 all-gather.2.cloned.1.call-update
  250.2 208.7 %reduce-scatter.5.cloned.1.call-done = bf16[32,4096]{1,0:T(8,128)(2,1)} async-done(((bf16[512,4096]{1,0:T(8,128)(2,1)}), bf16[32,4096]{1,0:T(8,128)(2,1)}) %reduce-scatter.5.cloned.1.call-update) | async-done | bytes 262160 | tf_op jit(solution)/shard_map/reduce_scatter | solution.py:42
  458.8 0.0 copy-done.1
  458.8 1.1 fusion.6
  460.0 1.3 multiply_reduce_fusion
  461.3 133.7 %all-gather.2.cloned.1.call-done = bf16[640,2,2,1536]{3,0,1,2:T(8,128)(2,1)} async-done(((bf16[40,2,2,1536]{3,0,1,2:T(8,128)(2,1)}), bf16[640,2,2,1536]{3,0,1,2:T(8,128)(2,1)}) %all-gather.2.cloned.1.call-update) | async-done | bytes 7864336 | tf_op jit(solution)/shard_map/all_gather | solution.py:88
  594.9 0.0 copy-start.5
  594.9 3.9 fusion
  598.9 0.9 copy-done.5
  599.8 0.0 copy-start.2
  599.8 2.7 fusion.5
  602.5 1.5 copy.44
  604.0 5.4 all-to-all-start.1
  609.3 0.0 copy-done.2
  609.3 1.0 fusion.20
  610.3 10.4 %all-to-all-done.1 = bf16[640,2,256]{2,1,0:T(2,128)(2,1)S(1)} async-done(((bf16[640,2,256]{2,1,0:T(2,128)(2,1)}), bf16[640,2,256]{2,1,0:T(2,128)(2,1)S(1)}, u32[]{:S(2)}, u32[]{:S(2)}) %all-to-all-start.1) | async-done | bytes 655392 | tf_op jit(solution)/shard_map/all_to_all | solution.py:96
  620.8 0.7 copy.58
  621.5 0.3 reshape.36
  621.7 1.9 fusion.24
  (3 shorter events, 0.1 us)
Async XLA Ops:
  7.2 27.8 %copy-start = (bf16[2,1536,256]{2,1,0:T(8,128)(2,1)S(1)}, bf16[2,1536,256]{2,1,0:T(8,128)(2,1)}, u32[]{:S(2)}) copy-start(bf16[2,1536,256]{2,1,0:T(8,128)(2,1)} %param.21) | copy-start | bytes 4718596
  7.2 240.9 %reduce-scatter.7.cloned.1.call-start = ((), (), s32[]{:S(2)}) async-start(), calls=%async_computation.6 | async-start | bytes 4177920
  38.7 1.1 copy-start.6
  38.7 420.2 %reduce-scatter.5.cloned.1.call-start = ((), (), s32[]{:S(2)}) async-start(), calls=%async_computation.4 | async-start | bytes 4456448 | tf_op jit(solution)/shard_map/reduce_scatter | solution.py:42
  47.6 200.5 %copy-start.3 = (bf16[40,2,1536]{2,1,0:T(2,128)(2,1)S(1)}, bf16[40,2,1536]{2,1,0:T(2,128)(2,1)}, u32[]{:S(2)}) copy-start(bf16[40,2,1536]{2,1,0:T(2,128)(2,1)} %param.18) | copy-start | bytes 737284
  47.6 200.5 %copy-start.4 = (bf16[40,2,1536]{2,1,0:T(2,128)(2,1)S(1)}, bf16[40,2,1536]{2,1,0:T(2,128)(2,1)}, u32[]{:S(2)}) copy-start(bf16[40,2,1536]{2,1,0:T(2,128)(2,1)} %param.17) | copy-start | bytes 737284
  47.6 411.3 %copy-start.1 = (f32[32,4096]{1,0:T(8,128)S(1)}, f32[32,4096]{1,0:T(8,128)}, u32[]{:S(2)}) copy-start(f32[32,4096]{1,0:T(8,128)} %param.13) | copy-start | bytes 1572868
  47.6 547.3 %all-gather.2.cloned.1.call-start = ((), (), s32[]{:S(2)}) async-start(), calls=%async_computation.5 | async-start | bytes 8355840 | tf_op jit(solution)/shard_map/all_gather | solution.py:88
  594.9 4.9 copy-start.5
  599.8 9.6 %copy-start.2 = (bf16[32,4096]{1,0:T(8,128)(2,1)S(1)}, bf16[32,4096]{1,0:T(8,128)(2,1)}, u32[]{:S(2)}) copy-start(bf16[32,4096]{1,0:T(8,128)(2,1)} %reduce-scatter.5.cloned.1.call-done) | copy-start | bytes 786436
  604.0 16.8 %all-to-all-start.1 = ((bf16[640,2,256]{2,1,0:T(2,128)(2,1)}), bf16[640,2,256]{2,1,0:T(2,128)(2,1)S(1)}, u32[]{:S(2)}, u32[]{:S(2)}) async-start(bf16[640,2,256]{2,1,0:T(2,128)(2,1)} %copy.44), calls=%async_computation.2 | async-start | bytes 1310720 | tf_op jit(solution)/shard_map/all_to_all | solution.py:96
Sparse Core Ops, SparseCore 0:
  38.8 209.2 reduce-scatter.6
  252.6 206.1 reduce-scatter.4
  462.0 132.8 all-gather.1
where the time goes:
time: 631 us; the launch traced here: 630 us
  waiting for transfers between devices  553 us (88%)
  matrix products  19.2 us (3%)
  blocking collectives  18.3 us (3%)
  between operations  13.8 us (2%)
  other arithmetic  11.8 us (2%)
  local copies, waits for them, and re-layouts  8.22 us (1%)
    reduce_scatter x1, waiting for transfers between devices, weight_update(): lax.psum_scatter(lax.dot_general(query_grad, attn_input, (((0,), (0,)), (...  209 us
    unnamed x4, waiting for transfers between devices  201 us
    all_gather x1, waiting for transfers between devices, expert_update(): part_rows = lax.all_gather(grads_pair, 'dp', axis=0, tiled=True)  134 us
    all_to_all x1, blocking collectives, expert_update(): lax.all_to_all(outgoing, 'expert', split_axis=1, concat_axis=0, tiled=True)  18.3 us
  transfers between devices with their start and end apart: 4, of which 4 were waited for; matrix products, arithmetic and copies ran while one was open for 2% of the time, Pallas kernels for 0%

commit v1 on v0

--- a/solution.py
+++ b/solution.py
@@ -85,7 +85,9 @@
         tiled=True,
     ).astype(jnp.float32)
     grads_pair = activation_grads(hidden, gate_saved, up_saved)
-    part_rows = lax.all_gather(grads_pair, "dp", axis=0, tiled=True)
+    part_rows = jnp.concatenate(
+        lax.all_to_all(jnp.stack([grads_pair] * lax.axis_size("dp")), "dp", 0, 0), axis=0
+    )
     total = jnp.einsum(
         "seh,ech->sec", part_rows[:, :, 0], gate_weight, preferred_element_type=jnp.float32
     )

time: 631 us -> 600 us (0.951)
  waiting for transfers between devices: 553 us -> 508 us
  starting transfers between devices: 5.5 us -> 15.7 us
    all_gather x1 -> x0, waiting for transfers between devices: 134 us -> none  [expert_update(): part_rows = lax.all_gather(grads_pair, 'dp', axis=0, tiled=True)]
    reduce_scatter x1, waiting for transfers between devices: 209 us -> 290 us  [weight_update(): lax.psum_scatter(lax.dot_general(query_grad, attn_input, (((0,), (0,)), (...]
    unnamed x4 -> x3, waiting for transfers between devices: 201 us -> 209 us
  transfers between devices with their start and end apart: 4 -> 4, of which waited for: 4 -> 3; matrix products, arithmetic and copies ran while one was open for 2% -> 2% of each run, Pallas kernels for 0% -> 0%
where the time goes in v1:
time: 600 us; the launch traced here: 599 us
  waiting for transfers between devices  508 us (85%)
  blocking collectives  18.3 us (3%)
  matrix products  16.6 us (3%)
  starting transfers between devices  15.7 us (3%)
  local copies, waits for them, and re-layouts  14.2 us (2%)
  between operations  14.2 us (2%)
  other arithmetic  12 us (2%)
    reduce_scatter x1, waiting for transfers between devices, weight_update(): lax.psum_scatter(lax.dot_general(query_grad, attn_input, (((0,), (0,)), (...  290 us
    unnamed x3, waiting for transfers between devices  209 us
    all_to_all x1, blocking collectives, expert_update(): lax.all_to_all(outgoing, 'expert', split_axis=1, concat_axis=0, tiled=True)  18.3 us
  transfers between devices with their start and end apart: 4, of which 3 were waited for; matrix products, arithmetic and copies ran while one was open for 2% of the time, Pallas kernels for 0%

profile of v1, /device:TPU:1, one launch (start us, length us, event | category | flops | bytes accessed | tf_op | source)
XLA Modules:
  0.0 599.5 jit_solution(9703269155314856137)
XLA Ops:
  7.2 0.0 copy-start
  7.2 0.0 reduce-scatter.7.cloned.1.call-start
  7.2 0.8 convert_reduce_fusion.1
  8.0 0.1 convolution_convert_fusion.3
  8.2 0.7 select_reduce_fusion.1
  8.9 0.7 multiply_add_fusion
  9.6 0.1 copy.39
  9.7 0.8 copy.40
  10.5 4.1 convert_reduce_fusion
  14.6 1.6 convolution_convert_fusion.2
  16.2 0.4 copy.41
  16.6 18.3 %all_to_all.38 = bf16[40,32,256]{2,0,1:T(8,128)(2,1)S(1)} all-to-all(bf16[40,32,256]{2,0,1:T(8,128)(2,1)S(1)} %copy.41), channel_id=1, replica_groups=mesh['expert'=16,'dp'=16] {'expert'}, dimensions={1} | all-to-all | bytes 1310720 | tf_op jit(solution)/shard_map/all_to_all | solution.py:78
  35.0 0.0 copy-done
  35.0 1.2 fusion.2
  36.2 2.5 copy.51
  38.7 0.0 copy-start.3
  38.7 0.0 copy-start.4
  38.7 0.0 reduce-scatter.7.cloned.1.call-update
  38.7 209.4 %reduce-scatter.7.cloned.1.call-done = bf16[40,3072]{1,0:T(8,128)(2,1)} async-done(((bf16[640,3072]{1,0:T(8,128)(2,1)}), bf16[40,3072]{1,0:T(8,128)(2,1)}) %reduce-scatter.7.cloned.1.call-update) | async-done | bytes 245776
  248.1 0.0 copy-done.3
  248.1 0.0 copy-done.4
  248.1 1.2 fusion.22
  249.4 4.1 stack.11
  253.5 0.0 copy-start.6
  253.5 6.1 %all-to-all-start.1 = ((bf16[16,40,2,2,1536]{4,1,2,3,0:T(8,128)(2,1)}), bf16[16,40,2,2,1536]{4,1,2,3,0:T(8,128)(2,1)}, u32[]{:S(2)}, u32[]{:S(2)}) async-start(bf16[16,40,2,2,1536]{4,1,2,3,0:T(8,128)(2,1)} %stack.11), calls=%async_computation.2 | async-start | bytes 15728640 | tf_op jit(solution)/shard_map/all_to_all | solution.py:89
  259.5 0.0 reduce-scatter.5.cloned.1.call-start
  259.6 0.0 copy-done.6
  259.6 7.8 %convolution_convert_fusion = bf16[512,4096]{1,0:T(8,128)(2,1)} fusion(bf16[768,512]{1,0:T(8,128)(2,1)S(1)} %copy-done.6, bf16[768,4096]{1,0:T(8,128)(2,1)} %param.11), kind=kOutput, calls=%fused_computation | convolution fusion | flops 3223322624 | bytes 11272192 | tf_op jit(solution)/shard_map/dot_general | solution.py:43
  267.5 0.0 copy-start.1
  267.5 0.0 reduce-scatter.5.cloned.1.call-update
  267.5 289.6 %reduce-scatter.5.cloned.1.call-done = bf16[32,4096]{1,0:T(8,128)(2,1)} async-done(((bf16[512,4096]{1,0:T(8,128)(2,1)}), bf16[32,4096]{1,0:T(8,128)(2,1)}) %reduce-scatter.5.cloned.1.call-update) | async-done | bytes 262160 | tf_op jit(solution)/shard_map/reduce_scatter | solution.py:42
  557.1 0.0 copy-done.1
  557.1 1.1 fusion.6
  558.2 1.3 multiply_reduce_fusion
  559.5 0.0 all-to-all-done.1
  559.5 3.9 copy.45
  563.4 0.0 copy-start.5
  563.4 2.7 fusion
  566.1 0.0 copy-done.5
  566.1 0.0 copy-start.2
  566.1 1.2 fusion.5
  567.3 1.5 copy.46
  568.9 9.5 %all-to-all-start.2 = ((bf16[640,2,256]{2,1,0:T(2,128)(2,1)}), bf16[640,2,256]{2,1,0:T(2,128)(2,1)S(1)}, u32[]{:S(2)}, u32[]{:S(2)}) async-start(bf16[640,2,256]{2,1,0:T(2,128)(2,1)} %copy.46), calls=%async_computation.3 | async-start | bytes 1310720 | tf_op jit(solution)/shard_map/all_to_all | solution.py:98
  578.4 0.0 copy-done.2
  578.4 2.0 fusion.20
  580.4 9.4 %all-to-all-done.2 = bf16[640,2,256]{2,1,0:T(2,128)(2,1)S(1)} async-done(((bf16[640,2,256]{2,1,0:T(2,128)(2,1)}), bf16[640,2,256]{2,1,0:T(2,128)(2,1)S(1)}, u32[]{:S(2)}, u32[]{:S(2)}) %all-to-all-start.2) | async-done | bytes 655392 | tf_op jit(solution)/shard_map/all_to_all | solution.py:98
  589.8 0.7 copy.60
  590.5 0.3 reshape.51
  590.7 1.9 fusion.24
  (4 shorter events, 0.1 us)
Async XLA Ops:
  7.2 27.8 %copy-start = (bf16[2,1536,256]{2,1,0:T(8,128)(2,1)S(1)}, bf16[2,1536,256]{2,1,0:T(8,128)(2,1)}, u32[]{:S(2)}) copy-start(bf16[2,1536,256]{2,1,0:T(8,128)(2,1)} %param.21) | copy-start | bytes 4718596
  7.2 240.9 %reduce-scatter.7.cloned.1.call-start = ((), (), s32[]{:S(2)}) async-start(), calls=%async_computation.6 | async-start | bytes 4177920
  38.7 209.4 %copy-start.3 = (bf16[40,2,1536]{2,1,0:T(2,128)(2,1)S(1)}, bf16[40,2,1536]{2,1,0:T(2,128)(2,1)}, u32[]{:S(2)}) copy-start(bf16[40,2,1536]{2,1,0:T(2,128)(2,1)} %param.18) | copy-start | bytes 737284
  38.7 209.4 %copy-start.4 = (bf16[40,2,1536]{2,1,0:T(2,128)(2,1)S(1)}, bf16[40,2,1536]{2,1,0:T(2,128)(2,1)}, u32[]{:S(2)}) copy-start(bf16[40,2,1536]{2,1,0:T(2,128)(2,1)} %param.17) | copy-start | bytes 737284
  253.5 6.1 %copy-start.6 = (bf16[768,512]{1,0:T(8,128)(2,1)S(1)}, bf16[768,512]{1,0:T(8,128)(2,1)}, u32[]{:S(2)}) copy-start(bf16[768,512]{1,0:T(8,128)(2,1)} %param.12) | copy-start | bytes 2359300
  253.5 306.0 %all-to-all-start.1 = ((bf16[16,40,2,2,1536]{4,1,2,3,0:T(8,128)(2,1)}), bf16[16,40,2,2,1536]{4,1,2,3,0:T(8,128)(2,1)}, u32[]{:S(2)}, u32[]{:S(2)}) async-start(bf16[16,40,2,2,1536]{4,1,2,3,0:T(8,128)(2,1)} %stack.11), calls=%async_computation.2 | async-start | bytes 15728640 | tf_op jit(solution)/shard_map/all_to_all | solution.py:89
  259.5 297.5 %reduce-scatter.5.cloned.1.call-start = ((), (), s32[]{:S(2)}) async-start(), calls=%async_computation.5 | async-start | bytes 4456448 | tf_op jit(solution)/shard_map/reduce_scatter | solution.py:42
  267.5 289.6 %copy-start.1 = (f32[32,4096]{1,0:T(8,128)S(1)}, f32[32,4096]{1,0:T(8,128)}, u32[]{:S(2)}) copy-start(f32[32,4096]{1,0:T(8,128)} %param.13) | copy-start | bytes 1572868
  563.4 2.8 copy-start.5
  566.1 12.3 %copy-start.2 = (bf16[32,4096]{1,0:T(8,128)(2,1)S(1)}, bf16[32,4096]{1,0:T(8,128)(2,1)}, u32[]{:S(2)}) copy-start(bf16[32,4096]{1,0:T(8,128)(2,1)} %reduce-scatter.5.cloned.1.call-done) | copy-start | bytes 786436
  568.9 20.9 %all-to-all-start.2 = ((bf16[640,2,256]{2,1,0:T(2,128)(2,1)}), bf16[640,2,256]{2,1,0:T(2,128)(2,1)S(1)}, u32[]{:S(2)}, u32[]{:S(2)}) async-start(bf16[640,2,256]{2,1,0:T(2,128)(2,1)} %copy.46), calls=%async_computation.3 | async-start | bytes 1310720 | tf_op jit(solution)/shard_map/all_to_all | solution.py:98
Sparse Core Ops, SparseCore 0:
  38.8 209.2 reduce-scatter.6
  267.6 289.4 reduce-scatter.4
